TPU v7x, 768 devices: a whole 4x8x12 slice. The times are simulated.
768 devices in a mesh: rep: 96 (over z, y), fsdp: 8 (over x, core).
Axes of the slice: x: 4, y: 8, z: 12, core: 2. Of those that a mesh axis runs over, the one named last changes fastest.
Arguments:
- deltas: bfloat16 [96, 48, 8192], P('rep', 'fsdp'), may hold values from -24 to 24, as said below
- momentum: float32 [48, 8192], P('fsdp'), may hold values from -6 to 6
- master: float32 [48, 8192], P('fsdp'), may hold values from -6 to 6
Outputs:
- new_momentum: float32 [48, 8192], P('fsdp')
- new_master: float32 [48, 8192], P('fsdp')
- full_weights: bfloat16 [48, 8192], replicated
Inputs may be any that keep to these rules, and one draw needn't show every extreme that they name: `deltas`: each replica's pseudo-gradient entries.
All inputs are finite; a program needn't handle non-finite values.
Results may differ from a plain program's by a relative error of at most 0.0004.
Values may be sent and summed in bfloat16 or wider, within the bound.
A program may use at most 32 MiB of HBM per device.

v0:
```python
import jax
import jax.numpy as jnp
from jax import lax
from jax.sharding import PartitionSpec as P

ITERS = 3


EPS = 1e-06


def outer_step(center, momentum, master):
    new_momentum = 0.9 * momentum + center
    new_master = master - 0.7 * (center + 0.9 * new_momentum)
    return (new_momentum, new_master)


def body(deltas, momentum, master):
    own = deltas[0]
    rows, width = own.shape
    entries = lax.axis_size("fsdp") * rows * width
    center = jnp.zeros((rows, width), jnp.float32)

    def weight_of(center):
        spread = own.astype(jnp.float32) - center
        squared = lax.psum(jnp.sum(spread * spread), "fsdp")
        return 1.0 / jnp.sqrt(squared / entries + EPS)

    def reweigh(center):
        weight = weight_of(center)
        numer, weight_sum = lax.psum((weight * own.astype(jnp.float32), weight), "rep")
        return numer / weight_sum

    for step in range(ITERS - 1):
        center = reweigh(center)
    median = reweigh(center)
    new_momentum, new_master = outer_step(median, momentum, master)
    full_weights = lax.all_gather(new_master.astype(jnp.bfloat16), "fsdp", axis=0, tiled=True)
    return (new_momentum, new_master, full_weights)


def solution(mesh):
    placed = (P("rep", "fsdp", None), P("fsdp", None), P("fsdp", None))
    return jax.shard_map(
        body,
        mesh=mesh,
        in_specs=placed,
        out_specs=(P("fsdp", None), P("fsdp", None), P()),
        check_vma=False,
    )
```

profile of v0, /device:TPU:1, one launch (start us, length us, event | category | flops | bytes accessed | tf_op | source)
XLA Modules:
  0.0 748.4 jit_solution(14089681605628994445)
XLA Ops:
  7.2 0.0 copy-start
  7.2 0.0 all-reduce.4.cloned.1.call-start
  7.2 1.6 fusion
  8.8 22.9 %psum.63 = f32[]{:T(128)} all-reduce(f32[]{:T(128)} %fusion), channel_id=1, replica_groups=mesh['rep'=96,'fsdp'=8] {'fsdp'}, use_global_device_ids=true, to_apply=%region_1.0 | all-reduce | flops 1 | bytes 8 | tf_op jit(solution)/shard_map/psum | solution.py:26
  32.4 0.0 copy-done
  32.4 0.7 convert_multiply_fusion.2
  33.2 0.0 all-reduce.4.cloned.1.call-update
  33.2 0.0 all-reduce.6.cloned.1.call-start
  33.2 172.5 %psum.65 = f32[]{:T(128)} all-reduce(f32[]{:T(128)S(6)} %sqrt.9), channel_id=1, replica_groups=mesh['rep'=96,'fsdp'=8] {'rep'}, use_global_device_ids=true, to_apply=%region_3.0 | all-reduce | flops 1 | bytes 8 | tf_op jit(solution)/shard_map/psum | solution.py:31
  205.7 42.1 %all-reduce.4.cloned.1.call-done = f32[6,8192]{1,0:T(8,128)} async-done(((f32[6,8192]{1,0:T(8,128)}), f32[6,8192]{1,0:T(8,128)}) %all-reduce.4.cloned.1.call-update) | async-done | bytes 196624 | tf_op jit(solution)/shard_map/psum | solution.py:31
  247.7 2.3 fusion.2
  250.0 19.6 %psum.66 = f32[]{:T(128)} all-reduce(f32[]{:T(128)} %fusion.2), channel_id=1, replica_groups=mesh['rep'=96,'fsdp'=8] {'fsdp'}, use_global_device_ids=true, to_apply=%region_5.0 | all-reduce | flops 1 | bytes 8 | tf_op jit(solution)/shard_map/psum | solution.py:26
  270.3 0.7 convert_multiply_fusion.1
  271.0 0.0 all-reduce.6.cloned.1.call-update
  271.0 0.0 all-reduce.8.cloned.1.call-start
  271.1 168.9 %psum.68 = f32[]{:T(128)} all-reduce(f32[]{:T(128)S(6)} %sqrt.10), channel_id=1, replica_groups=mesh['rep'=96,'fsdp'=8] {'rep'}, use_global_device_ids=true, to_apply=%region_7.0 | all-reduce | flops 1 | bytes 8 | tf_op jit(solution)/shard_map/psum | solution.py:31
  440.0 42.6 %all-reduce.6.cloned.1.call-done = f32[6,8192]{1,0:T(8,128)} async-done(((f32[6,8192]{1,0:T(8,128)}), f32[6,8192]{1,0:T(8,128)}) %all-reduce.6.cloned.1.call-update) | async-done | bytes 196624 | tf_op jit(solution)/shard_map/psum | solution.py:31
  482.6 2.3 fusion.4
  484.9 19.4 %psum.69 = f32[]{:T(128)} all-reduce(f32[]{:T(128)} %fusion.4), channel_id=1, replica_groups=mesh['rep'=96,'fsdp'=8] {'fsdp'}, use_global_device_ids=true, to_apply=%region_9.0 | all-reduce | flops 1 | bytes 8 | tf_op jit(solution)/shard_map/psum | solution.py:26
  504.9 0.0 copy-start.1
  504.9 0.0 copy-start.2
  505.0 0.7 convert_multiply_fusion
  505.7 0.0 all-reduce.8.cloned.1.call-update
  505.7 168.8 %psum.71 = f32[]{:T(128)} all-reduce(f32[]{:T(128)S(6)} %sqrt.11), channel_id=1, replica_groups=mesh['rep'=96,'fsdp'=8] {'rep'}, use_global_device_ids=true, to_apply=%region_11.0 | all-reduce | flops 1 | bytes 8 | tf_op jit(solution)/shard_map/psum | solution.py:31
  674.6 42.7 %all-reduce.8.cloned.1.call-done = f32[6,8192]{1,0:T(8,128)} async-done(((f32[6,8192]{1,0:T(8,128)}), f32[6,8192]{1,0:T(8,128)}) %all-reduce.8.cloned.1.call-update) | async-done | bytes 196624 | tf_op jit(solution)/shard_map/psum | solution.py:31
  717.3 0.0 copy-done.1
  717.3 0.0 copy-done.2
  717.3 2.5 convert_bitcast_fusion
  719.7 21.0 %all-gather = bf16[8,6,8192]{2,1,0:T(8,128)(2,1)S(1)} all-gather(bf16[1,6,8192]{2,1,0:T(8,128)(2,1)S(1)} %get-tuple-element.3), channel_id=1, replica_groups=mesh['rep'=96,'fsdp'=8] {'fsdp'}, dimensions={0}, use_global_device_ids=true | all-gather | bytes 884736 | tf_op jit(solution)/shard_map/all_gather | solution.py:38
  740.7 1.2 reshape.10
Async XLA Ops:
  7.2 25.3 %copy-start = (bf16[1,6,8192]{2,1,0:T(8,128)(2,1)S(1)}, bf16[1,6,8192]{2,1,0:T(8,128)(2,1)}, u32[]{:S(2)}) copy-start(bf16[1,6,8192]{2,1,0:T(8,128)(2,1)} %param.3) | copy-start | bytes 294916
  7.2 240.6 %all-reduce.4.cloned.1.call-start = ((), (), s32[]{:S(2)}) async-start(), calls=%async_computation | async-start | bytes 524288 | tf_op jit(solution)/shard_map/psum | solution.py:31
  33.2 449.4 %all-reduce.6.cloned.1.call-start = ((), (), s32[]{:S(2)}) async-start(), calls=%async_computation.1 | async-start | bytes 524288 | tf_op jit(solution)/shard_map/psum | solution.py:31
  271.0 446.2 %all-reduce.8.cloned.1.call-start = ((), (), s32[]{:S(2)}) async-start(), calls=%async_computation.2 | async-start | bytes 524288 | tf_op jit(solution)/shard_map/psum | solution.py:31
  504.9 212.3 %copy-start.1 = (f32[6,8192]{1,0:T(8,128)S(1)}, f32[6,8192]{1,0:T(8,128)}, u32[]{:S(2)}) copy-start(f32[6,8192]{1,0:T(8,128)} %param.5) | copy-start | bytes 589828
  504.9 212.3 %copy-start.2 = (f32[6,8192]{1,0:T(8,128)S(1)}, f32[6,8192]{1,0:T(8,128)}, u32[]{:S(2)}) copy-start(f32[6,8192]{1,0:T(8,128)} %param.4) | copy-start | bytes 589828
Sparse Core Ops, SparseCore 0:
  33.3 214.3 all-reduce.3
  271.2 211.3 all-reduce.5
  505.8 211.3 all-reduce.7
where the time goes:
time: 749 us; the launch traced here: 748 us
  blocking collectives  593 us (79%)
  waiting for transfers between devices  127 us (17%)
  between operations  15.9 us (2%)
  other arithmetic  10.8 us (1%)
    psum x3, blocking collectives, reweigh(): lax.psum((weight * own.astype(jnp.float32), weight), 'rep')  510 us
    psum x3, waiting for transfers between devices, reweigh(): lax.psum((weight * own.astype(jnp.float32), weight), 'rep')  127 us
    psum x3, blocking collectives, weight_of(): squared = lax.psum(jnp.sum(spread * spread), 'fsdp')  61.8 us
    all_gather x1, blocking collectives, body(): lax.all_gather(new_master.astype(jnp.bfloat16), 'fsdp', axis=0, tiled=True)  21 us
  transfers between devices with their start and end apart: 3, of which 3 were waited for; matrix products, arithmetic and copies ran while one was open for 0% of the time, Pallas kernels for 0%

commit v1 on v0

v1 whole, which is shorter than its diff:
```python
import functools

import jax
import jax.numpy as jnp
from jax import lax
from jax.experimental import pallas as pl
from jax.experimental.pallas import tpu as pltpu
from jax.sharding import PartitionSpec as P

ITERS = 3
EPS = 1e-06
NY = 8
LANES = 128
MESH = pl.DeviceIdType.MESH
F32, BF16 = jnp.float32, jnp.bfloat16


def split3(value):
    high = value.astype(BF16)
    rest = value - high.astype(F32)
    mid = rest.astype(BF16)
    low = (rest - mid.astype(F32)).astype(BF16)
    return high, mid, low


def kernel(
    nf, nz, delta, mom, mas, nm, ns, fw,
    own, ra, rf, tb, zb, zq, xs, ys, zs, cd, cn, nd, wb, wf,
    local_sem, a_sem, b_sem, x_sem, y_sem, z_sem, cz_sem, cy_send, cy_recv, w_send, w_recv,
):
    rows, width = own.shape
    block = width // NY
    halves = nz // rows
    chunk = block // halves
    tiles = block // LANES
    parts = chunk // LANES
    reps = NY * nz
    entries = nf * rows * width

    rep, f = lax.axis_index("rep"), lax.axis_index("fsdp")
    y, z = lax.rem(rep, NY), lax.div(rep, NY)

    def peers(axis, n, me, visit):
        def step(i, carry):
            half = lax.div(i + 1, 2)
            place = lax.rem(me + n // 2 + half * (2 * lax.rem(i, 2) - 1) + n, n)
            if axis == "x":
                device = (rep, place)
            elif axis == "y":
                device = (z * NY + place, f)
            else:
                device = (place * NY + y, f)
            visit(device, place)
            return carry

        lax.fori_loop(0, n - 1, step, 0)

    def send(src, dst, send_sem, recv_sem, device):
        pltpu.make_async_remote_copy(
            src_ref=src, dst_ref=dst, send_sem=send_sem, recv_sem=recv_sem,
            device_id=device, device_id_type=MESH,
        ).start()

    def drain(ref, sem):
        pltpu.make_async_copy(ref, ref, sem).wait()

    own_copy = pltpu.make_async_copy(delta.at[0], own, local_sem.at[0])
    own_copy.start()
    mine = pl.ds(pl.multiple_of(y * block, block), block)
    block_copy = pltpu.make_async_copy(delta.at[0, :, mine], ra.at[y], local_sem.at[1])
    block_copy.start()

    barrier = pltpu.get_barrier_semaphore()

    def greet(device, place):
        pl.semaphore_signal(barrier, inc=1, device_id=device, device_id_type=MESH)

    peers("x", nf, f, greet)
    peers("y", NY, y, greet)
    peers("z", nz, z, greet)
    pl.semaphore_wait(barrier, nf + NY + nz - 3)

    def send_a(device, place):
        columns = pl.ds(pl.multiple_of(place * block, block), block)
        send(delta.at[0, :, columns], ra.at[y], a_sem.at[0], a_sem.at[1], device)

    peers("y", NY, y, send_a)

    def exchange(axis, n, me, buffer, sems, row):
        buffer[me] = row
        peers(axis, n, me, lambda device, place: send(buffer.at[me], buffer.at[me], sems.at[0], sems.at[1], device))
        drain(buffer.at[pl.ds(0, n - 1)], sems.at[1])
        return jnp.sum(buffer[...], axis=0)

    def x_stage(k, row):
        return exchange("x", nf, f, xs.at[k], x_sem.at[k], row)

    def y_stage(k, row):
        return exchange("y", NY, y, ys.at[k], y_sem.at[k], row)

    def z_stage(k, row):
        return exchange("z", nz, z, zs.at[k], z_sem.at[k], row)

    lane = lax.broadcasted_iota(jnp.int32, (1, LANES), 1)

    own_copy.wait()
    value = own[...].astype(F32)
    squared = jnp.sum(jnp.sum(value * value, axis=0, keepdims=True), axis=1, keepdims=True)
    row = jnp.where(lane == rep, squared, 0.0)
    row = y_stage(0, x_stage(0, row))

    block_copy.wait()
    drain(ra.at[pl.ds(0, NY - 1)], a_sem.at[1])
    for k in range(NY):
        arrived = ra[k].astype(F32)
        for j in range(tiles):
            rf[pl.ds(8 * (j * NY + k), rows), :] = arrived[:, j * LANES : (j + 1) * LANES]
    for r in range(rows):
        for j in range(tiles):
            column = pl.ds(j * LANES, LANES)
            tb[r, :, column] = rf[pl.ds(8 * j * NY + r, NY, stride=8), :].astype(BF16)

    def piece(place):
        columns = pl.ds(pl.multiple_of(lax.rem(place, halves) * chunk, chunk), chunk)
        return tb.at[lax.div(place, halves), :, columns]

    peers("z", nz, z, lambda device, place: send(piece(place), zb.at[z], b_sem.at[0], b_sem.at[1], device))
    zb[z] = piece(z)[...]
    zq[pl.ds(reps, LANES - reps), :] = jnp.zeros((LANES - reps, LANES), F32)

    row = z_stage(0, row)
    drain(zb.at[pl.ds(0, nz - 1)], b_sem.at[1])
    held = zb[...].reshape(reps, chunk)

    def center_of(squared):
        weight = jnp.where(lane < reps, 1.0 / jnp.sqrt(squared / entries + EPS), 0.0)
        share = weight / jnp.sum(weight, axis=1, keepdims=True)
        left = jnp.concatenate(split3(share), axis=0)[:, :reps]
        return jnp.sum(jnp.dot(left, held, preferred_element_type=F32), axis=0, keepdims=True)

    center = center_of(row)
    for k in range(1, ITERS):
        spread = held.astype(F32) - center
        spread = spread * spread
        total = spread[:, :LANES]
        for part in range(1, parts):
            total = total + spread[:, part * LANES : (part + 1) * LANES]
        zq[pl.ds(0, reps), :] = total
        row = lax.dot_general(
            jnp.ones((8, LANES), F32), zq[...], (((1,), (1,)), ((), ())),
            precision=lax.Precision.HIGHEST, preferred_element_type=F32,
        )[:1]
        center = center_of(z_stage(k, y_stage(k, x_stage(k, row))))

    for part in range(parts):
        cd[y, z, pl.ds(part, 1), :] = center[:, part * LANES : (part + 1) * LANES]
    peers("z", nz, z, lambda device, place: send(cd.at[y, z], cd.at[y, z], cz_sem.at[0], cz_sem.at[1], device))
    drain(cd.at[0, pl.ds(0, nz - 1)], cz_sem.at[1])
    peers("y", NY, y, lambda device, place: send(cd.at[y], cd.at[y], cy_send.at[0], cy_recv.at[y], device))

    def update(i, carry):
        half = lax.div(i, 2) + lax.rem(i, 2)
        b = lax.rem(y + half * (1 - 2 * lax.rem(i, 2)) + NY, NY)

        @pl.when(i > 0)
        def _():
            drain(cd.at[b], cy_recv.at[b])

        for k in range(nz):
            cn[pl.ds(k * parts, parts), :] = cd[b, k]
        for j in range(tiles):
            here = pl.ds(pl.multiple_of(b * block + j * LANES, LANES), LANES)
            there = pl.ds(j, rows, stride=tiles)
            c = cn[there, :]
            momentum = 0.9 * mom[:, here] + c
            master = mas[:, here] - 0.7 * (c + 0.9 * momentum)
            nm[:, here] = momentum
            ns[:, here] = master
            nd[there, :] = master
        wb[f, b] = nd[...].astype(BF16)
        peers("x", nf, f, lambda device, place: send(wb.at[f, b], wb.at[f, b], w_send.at[0], w_recv.at[b], device))
        return carry

    lax.fori_loop(0, NY, update, 0)

    def place_weights(i, carry):
        half = lax.div(i, 2) + lax.rem(i, 2)
        b = lax.rem(y + half * (1 - 2 * lax.rem(i, 2)) + NY, NY)
        drain(wb.at[pl.ds(0, nf - 1), b], w_recv.at[b])
        for g in range(nf):
            dense = wb[g, b].astype(F32)
            for r in range(rows):
                wf[pl.ds(g * rows + r, tiles, stride=nf * rows), :] = dense[r * tiles : (r + 1) * tiles]
        for j in range(tiles):
            here = pl.ds(pl.multiple_of(b * block + j * LANES, LANES), LANES)
            fw[:, here] = wf[pl.ds(j * nf * rows, nf * rows), :].astype(BF16)
        return carry

    lax.fori_loop(0, NY, place_weights, 0)

    drain(ra.at[pl.ds(0, NY - 1)], a_sem.at[0])
    drain(zb.at[pl.ds(0, nz - 1)], b_sem.at[0])
    for k in range(ITERS):
        drain(xs.at[k, pl.ds(0, nf - 1)], x_sem.at[k, 0])
        drain(ys.at[k, pl.ds(0, NY - 1)], y_sem.at[k, 0])
        drain(zs.at[k, pl.ds(0, nz - 1)], z_sem.at[k, 0])
    drain(cd.at[0, pl.ds(0, nz - 1)], cz_sem.at[0])
    drain(cd.at[pl.ds(0, NY - 1)], cy_send.at[0])
    drain(wb.at[pl.ds(0, nf - 1)], w_send.at[0])


def solution(mesh):
    nf, nz = mesh.shape["fsdp"], mesh.shape["rep"] // NY

    def body(deltas, momentum, master):
        _, rows, width = deltas.shape
        block = width // NY
        chunk = block * rows // nz
        parts, tiles = chunk // LANES, block // LANES
        vmem = pl.BlockSpec(memory_space=pltpu.VMEM)
        dma = pltpu.SemaphoreType.DMA
        return pl.pallas_call(
            functools.partial(kernel, nf, nz),
            out_shape=(
                jax.ShapeDtypeStruct((rows, width), F32),
                jax.ShapeDtypeStruct((rows, width), F32),
                jax.ShapeDtypeStruct((nf * rows, width), BF16),
            ),
            in_specs=[pl.BlockSpec(memory_space=pl.ANY), vmem, vmem],
            out_specs=(vmem, vmem, vmem),
            scratch_shapes=[
                pltpu.VMEM((rows, width), BF16),
                pltpu.VMEM((NY, rows, block), BF16),
                pltpu.VMEM((tiles * NY * 8, LANES), F32),
                pltpu.VMEM((rows, NY, block), BF16),
                pltpu.VMEM((nz, NY, chunk), BF16),
                pltpu.VMEM((LANES, LANES), F32),
                pltpu.VMEM((ITERS, nf, 1, LANES), F32),
                pltpu.VMEM((ITERS, NY, 1, LANES), F32),
                pltpu.VMEM((ITERS, nz, 1, LANES), F32),
                pltpu.VMEM((NY, nz, parts, LANES), F32),
                pltpu.VMEM((rows * tiles, LANES), F32),
                pltpu.VMEM((rows * tiles, LANES), F32),
                pltpu.VMEM((nf, NY, rows * tiles, LANES), BF16),
                pltpu.VMEM((tiles * nf * rows, LANES), F32),
                dma((2,)),
                dma((2,)),
                dma((2,)),
                dma((ITERS, 2)),
                dma((ITERS, 2)),
                dma((ITERS, 2)),
                dma((2,)),
                dma((1,)),
                dma((NY,)),
                dma((1,)),
                dma((NY,)),
            ],
            compiler_params=pltpu.CompilerParams(collective_id=0, has_side_effects=True),
        )(deltas, momentum, master)

    placed = (P("rep", "fsdp", None), P("fsdp", None), P("fsdp", None))
    return jax.shard_map(
        body,
        mesh=mesh,
        in_specs=placed,
        out_specs=(P("fsdp", None), P("fsdp", None), P()),
        check_vma=False,
    )
```

time: 749 us -> 87.6 us (0.12)
  blocking collectives: 593 us -> 0 us
  waiting for transfers between devices: 127 us -> 0 us
  Pallas kernels: 0 us -> 82.5 us
  between operations: 15.9 us -> 0.65 us
  other arithmetic: 10.8 us -> 0 us
    psum x6 -> x0, blocking collectives: 572 us -> none  [the longest x3 510 us: reweigh(): lax.psum((weight * own.astype(jnp.float32), weight), 'rep')]
    psum x3 -> x0, waiting for transfers between devices: 127 us -> none  [reweigh(): lax.psum((weight * own.astype(jnp.float32), weight), 'rep')]
    pallas_call x0 -> x1, Pallas kernels: none -> 82.5 us  [body(): pl.pallas_call(functools.partial(kernel, nf, nz), out_shape=(jax.ShapeDty...]
    all_gather x1 -> x0, blocking collectives: 21 us -> none  [body(): lax.all_gather(new_master.astype(jnp.bfloat16), 'fsdp', axis=0, tiled=True)]
  transfers between devices with their start and end apart: 3 -> 0, of which waited for: 3 -> 0; matrix products, arithmetic and copies ran while one was open for 0% -> 0% of each run, Pallas kernels for 0% -> 0%
where the time goes in v1:
time: 87.6 us; the launch traced here: 87.4 us
  Pallas kernels  82.5 us (94%)
  local copies, waits for them, and re-layouts  4.3 us (5%)
    pallas_call x1, Pallas kernels, body(): pl.pallas_call(functools.partial(kernel, nf, nz), out_shape=(jax.ShapeDty...  82.5 us
    unnamed x5, local copies, waits for them, and re-layouts  4.3 us

profile of v1, /device:TPU:1, one launch (start us, length us, event | category | flops | bytes accessed | tf_op | source)
XLA Modules:
  0.0 87.4 jit_solution(2954016278521241908)
XLA Ops:
  0.6 82.5 %shard_map.58 = (f32[6,8192]{1,0:T(8,128)}, f32[6,8192]{1,0:T(8,128)}, bf16[48,8192]{1,0:T(8,128)(2,1)}) custom-call(bf16[1,6,8192]{2,1,0:T(8,128)(2,1)} %delta.1, f32[6,8192]{1,0:T(8,128)} %mom.1, f32[6,8192]{1,0:T(8,128)} %mas.1), custom_call_target="tpu_custom_call" | custom-call | tf_op jit(solution)/shard_map/pallas_call | solution.py:222
  83.1 0.0 copy-start
  83.1 1.7 %copy.9 = f32[6,8192]{1,0:T(8,128)} copy(f32[6,8192]{1,0:T(8,128)} %get-tuple-element.6) | data formatting | bytes 393216
  84.9 1.7 %copy.10 = f32[6,8192]{1,0:T(8,128)} copy(f32[6,8192]{1,0:T(8,128)} %get-tuple-element.7) | data formatting | bytes 393216
  86.5 0.0 copy-done
  86.5 0.9 %copy.11 = bf16[48,8192]{1,0:T(8,128)(2,1)} copy(bf16[48,8192]{1,0:T(8,128)(2,1)S(1)} %copy-done) | data formatting | bytes 1572864
Async XLA Ops:
  83.1 3.4 %copy-start = (bf16[48,8192]{1,0:T(8,128)(2,1)S(1)}, bf16[48,8192]{1,0:T(8,128)(2,1)}, u32[]{:S(2)}) copy-start(bf16[48,8192]{1,0:T(8,128)(2,1)} %get-tuple-element.8) | copy-start | bytes 2359300

commit v2 on v1

v2 whole, which is shorter than its diff:
```python
import functools

import jax
import jax.numpy as jnp
from jax import lax
from jax.experimental import pallas as pl
from jax.experimental.pallas import tpu as pltpu
from jax.sharding import PartitionSpec as P

ITERS = 3
EPS = 1e-06
NY = 8
LANES = 128
MESH = pl.DeviceIdType.MESH
F32, BF16 = jnp.float32, jnp.bfloat16


def split3(value):
    high = value.astype(BF16)
    rest = value - high.astype(F32)
    mid = rest.astype(BF16)
    low = (rest - mid.astype(F32)).astype(BF16)
    return high, mid, low


def kernel(
    nf, nz, delta, mom_in, mas_in, nm_out, ns_out, fw_out,
    own, mom, mas, nm, ns, fw, ra, rf, tb, zb, zq, ps, zs, cd, cn, nd, wb, wf,
    local_sem, out_sem, a_sem, b_sem, p_sem, z_sem, cz_sem, cy_send, cy_recv, w_send, w_recv, v_send, v_recv,
):
    rows, width = own.shape
    block = width // NY
    halves = nz // rows
    chunk = block // halves
    tiles = block // LANES
    parts = chunk // LANES
    reps = NY * nz
    entries = nf * rows * width

    rep, f = lax.axis_index("rep"), lax.axis_index("fsdp")
    y, z = lax.rem(rep, NY), lax.div(rep, NY)

    x, core = lax.div(f, 2), lax.rem(f, 2)
    plane = y * nf + f
    sibling = (rep, f + 1 - 2 * core)

    def peers(axis, visit):
        n = {"x": nf // 2, "y": NY, "z": nz, "plane": NY * nf}[axis]
        me = {"x": x, "y": y, "z": z, "plane": plane}[axis]

        def step(i, carry):
            half = lax.div(i + 1, 2)
            place = lax.rem(me + n // 2 + half * (2 * lax.rem(i, 2) - 1) + n, n)
            if axis == "x":
                device = (rep, 2 * place + core)
            elif axis == "y":
                device = (z * NY + place, f)
            elif axis == "z":
                device = (place * NY + y, f)
            else:
                device = (z * NY + lax.div(place, nf), lax.rem(place, nf))
            visit(device, place)
            return carry

        lax.fori_loop(0, n - 1, step, 0)

    def send(src, dst, send_sem, recv_sem, device):
        pltpu.make_async_remote_copy(
            src_ref=src, dst_ref=dst, send_sem=send_sem, recv_sem=recv_sem,
            device_id=device, device_id_type=MESH,
        ).start()

    def drain(ref, sem):
        pltpu.make_async_copy(ref, ref, sem).wait()

    own_copy = pltpu.make_async_copy(delta.at[0], own, local_sem.at[0])
    own_copy.start()
    mine = pl.ds(pl.multiple_of(y * block, block), block)
    block_copy = pltpu.make_async_copy(delta.at[0, :, mine], ra.at[y], local_sem.at[1])
    block_copy.start()

    barrier = pltpu.get_barrier_semaphore()

    def greet(device, place):
        pl.semaphore_signal(barrier, inc=1, device_id=device, device_id_type=MESH)

    peers("plane", greet)
    peers("z", greet)

    mom_copy = pltpu.make_async_copy(mom_in, mom, local_sem.at[2])
    mas_copy = pltpu.make_async_copy(mas_in, mas, local_sem.at[3])
    lane = lax.broadcasted_iota(jnp.int32, (1, LANES), 1)
    own_copy.wait()
    value = own[...].astype(F32)
    squared = jnp.sum(jnp.sum(value * value, axis=0, keepdims=True), axis=1, keepdims=True)
    row = jnp.where(lane == rep, squared, 0.0)
    pl.semaphore_wait(barrier, NY * nf + nz - 2)

    def send_a(device, place):
        columns = pl.ds(pl.multiple_of(place * block, block), block)
        send(own.at[:, columns], ra.at[y], a_sem.at[0], a_sem.at[1], device)

    def exchange(axis, n, me, buffer, sems, row):
        buffer[me] = row
        peers(axis, lambda device, place: send(buffer.at[me], buffer.at[me], sems.at[0], sems.at[1], device))

        def total():
            drain(buffer.at[pl.ds(0, n - 1)], sems.at[1])
            return jnp.sum(buffer[...], axis=0)

        return total

    def plane_stage(k, row):
        return exchange("plane", NY * nf, plane, ps.at[k], p_sem.at[k], row)

    def z_stage(k, row):
        return exchange("z", nz, z, zs.at[k], z_sem.at[k], row)

    peers("y", send_a)
    total = plane_stage(0, row)
    mom_copy.start()
    mas_copy.start()

    block_copy.wait()
    drain(ra.at[pl.ds(0, NY - 1)], a_sem.at[1])
    for k in range(NY):
        arrived = ra[k].astype(F32)
        for j in range(tiles):
            rf[pl.ds(8 * (j * NY + k), rows), :] = arrived[:, j * LANES : (j + 1) * LANES]
    for r in range(rows):
        for j in range(tiles):
            column = pl.ds(j * LANES, LANES)
            tb[r, :, column] = rf[pl.ds(8 * j * NY + r, NY, stride=8), :].astype(BF16)

    def piece(place):
        columns = pl.ds(pl.multiple_of(lax.rem(place, halves) * chunk, chunk), chunk)
        return tb.at[lax.div(place, halves), :, columns]

    peers("z", lambda device, place: send(piece(place), zb.at[z], b_sem.at[0], b_sem.at[1], device))
    total = z_stage(0, total())
    zb[z] = piece(z)[...]
    zq[pl.ds(reps, LANES - reps), :] = jnp.zeros((LANES - reps, LANES), F32)

    row = total()
    drain(zb.at[pl.ds(0, nz - 1)], b_sem.at[1])
    held = zb[...].reshape(reps, chunk)

    def center_of(squared):
        weight = jnp.where(lane < reps, 1.0 / jnp.sqrt(squared / entries + EPS), 0.0)
        share = weight / jnp.sum(weight, axis=1, keepdims=True)
        left = jnp.concatenate(split3(share), axis=0)[:, :reps]
        return jnp.sum(jnp.dot(left, held, preferred_element_type=F32), axis=0, keepdims=True)

    def iterate(k, center):
        spread = held.astype(F32) - center
        spread = spread * spread
        partial = spread[:, :LANES]
        for part in range(1, parts):
            partial = partial + spread[:, part * LANES : (part + 1) * LANES]
        zq[pl.ds(0, reps), :] = partial
        row = lax.dot_general(
            jnp.ones((8, LANES), F32), zq[...], (((1,), (1,)), ((), ())),
            precision=lax.Precision.HIGHEST, preferred_element_type=F32,
        )[:1]
        return center_of(z_stage(k, plane_stage(k, row)())())

    center = lax.fori_loop(1, ITERS, iterate, center_of(row))

    for part in range(parts):
        cd[y, z, pl.ds(part, 1), :] = center[:, part * LANES : (part + 1) * LANES]
    peers("z", lambda device, place: send(cd.at[y, z], cd.at[y, z], cz_sem.at[0], cz_sem.at[1], device))
    mom_copy.wait()
    mas_copy.wait()
    drain(cd.at[0, pl.ds(0, nz - 1)], cz_sem.at[1])
    peers("y", lambda device, place: send(cd.at[y], cd.at[y], cy_send.at[0], cy_recv.at[y], device))

    def nearest(i):
        half = lax.div(i, 2) + lax.rem(i, 2)
        return lax.rem(y + half * (1 - 2 * lax.rem(i, 2)) + NY, NY)

    def out_copies(b):
        columns = pl.ds(pl.multiple_of(b * block, block), block)
        return [
            pltpu.make_async_copy(ref.at[:, columns], out.at[:, columns], out_sem.at[at, b])
            for at, (ref, out) in enumerate(((nm, nm_out), (ns, ns_out), (fw, fw_out)))
        ]

    def update(i, carry):
        b = nearest(i)

        @pl.when(i > 0)
        def _():
            drain(cd.at[b], cy_recv.at[b])

        for k in range(nz):
            cn[pl.ds(k * parts, parts), :] = cd[b, k]
        for j in range(tiles):
            here = pl.ds(pl.multiple_of(b * block + j * LANES, LANES), LANES)
            there = pl.ds(j, rows, stride=tiles)
            c = cn[there, :]
            momentum = 0.9 * mom[:, here] + c
            master = mas[:, here] - 0.7 * (c + 0.9 * momentum)
            nm[:, here] = momentum
            ns[:, here] = master
            nd[there, :] = master
        wb[f, b] = nd[...].astype(BF16)
        peers("x", lambda device, place: send(wb.at[f, b], wb.at[f, b], w_send.at[0], w_recv.at[b], device))
        send(wb.at[f, b], wb.at[f, b], v_send.at[0], v_recv.at[b], sibling)
        for copy in out_copies(b)[:2]:
            copy.start()
        return carry

    lax.fori_loop(0, NY, update, 0)

    def forward(i, carry):
        b = nearest(i)
        drain(wb.at[pl.ds(0, nf // 2 - 1), b], w_recv.at[b])

        def step(k, carry):
            g = 2 * lax.rem(x + 1 + k, nf // 2) + core
            send(wb.at[g, b], wb.at[g, b], v_send.at[0], v_recv.at[b], sibling)
            return carry

        return lax.fori_loop(0, nf // 2 - 1, step, carry)

    lax.fori_loop(0, NY, forward, 0)

    def place_weights(i, carry):
        b = nearest(i)
        drain(wb.at[pl.ds(0, nf // 2), b], v_recv.at[b])
        for g in range(nf):
            dense = wb[g, b].astype(F32)
            for r in range(rows):
                wf[pl.ds(g * rows + r, tiles, stride=nf * rows), :] = dense[r * tiles : (r + 1) * tiles]
        for j in range(tiles):
            here = pl.ds(pl.multiple_of(b * block + j * LANES, LANES), LANES)
            fw[:, here] = wf[pl.ds(j * nf * rows, nf * rows), :].astype(BF16)
        out_copies(b)[2].start()
        return carry

    lax.fori_loop(0, NY, place_weights, 0)

    def leave(i, carry):
        for copy in out_copies(i):
            copy.wait()
        return carry

    lax.fori_loop(0, NY, leave, 0)
    drain(ra.at[pl.ds(0, NY - 1)], a_sem.at[0])
    drain(zb.at[pl.ds(0, nz - 1)], b_sem.at[0])
    for k in range(ITERS):
        drain(ps.at[k, pl.ds(0, NY * nf - 1)], p_sem.at[k, 0])
        drain(zs.at[k, pl.ds(0, nz - 1)], z_sem.at[k, 0])
    drain(cd.at[0, pl.ds(0, nz - 1)], cz_sem.at[0])
    drain(cd.at[pl.ds(0, NY - 1)], cy_send.at[0])
    drain(wb.at[pl.ds(0, nf // 2 - 1)], w_send.at[0])
    drain(wb.at[pl.ds(0, nf // 2)], v_send.at[0])


def copy_kernel(count, *refs):
    sems = refs[-1]
    copies = [pltpu.make_async_copy(refs[i], refs[count + i], sems.at[i]) for i in range(count)]
    for copy in copies:
        copy.start()
    for copy in copies:
        copy.wait()


def solution(mesh):
    nf, nz = mesh.shape["fsdp"], mesh.shape["rep"] // NY

    def body(deltas, momentum, master):
        _, rows, width = deltas.shape
        block = width // NY
        chunk = block * rows // nz
        parts, tiles = chunk // LANES, block // LANES
        anywhere = pl.BlockSpec(memory_space=pl.ANY)
        dma = pltpu.SemaphoreType.DMA
        outs = (
            jax.ShapeDtypeStruct((rows, width), F32),
            jax.ShapeDtypeStruct((rows, width), F32),
            jax.ShapeDtypeStruct((nf * rows, width), BF16),
        )
        results = pl.pallas_call(
            functools.partial(kernel, nf, nz),
            out_shape=outs,
            in_specs=[pl.BlockSpec(memory_space=pltpu.HBM)] * 3,
            out_specs=(anywhere,) * 3,
            scratch_shapes=[
                pltpu.VMEM((rows, width), BF16),
                pltpu.VMEM((rows, width), F32),
                pltpu.VMEM((rows, width), F32),
                pltpu.VMEM((rows, width), F32),
                pltpu.VMEM((rows, width), F32),
                pltpu.VMEM((nf * rows, width), BF16),
                pltpu.VMEM((NY, rows, block), BF16),
                pltpu.VMEM((tiles * NY * 8, LANES), F32),
                pltpu.VMEM((rows, NY, block), BF16),
                pltpu.VMEM((nz, NY, chunk), BF16),
                pltpu.VMEM((LANES, LANES), F32),
                pltpu.VMEM((ITERS, NY * nf, 1, LANES), F32),
                pltpu.VMEM((ITERS, nz, 1, LANES), F32),
                pltpu.VMEM((NY, nz, parts, LANES), F32),
                pltpu.VMEM((rows * tiles, LANES), F32),
                pltpu.VMEM((rows * tiles, LANES), F32),
                pltpu.VMEM((nf, NY, rows * tiles, LANES), BF16),
                pltpu.VMEM((tiles * nf * rows, LANES), F32),
                dma((4,)),
                dma((3, NY)),
                dma((2,)),
                dma((2,)),
                dma((ITERS, 2)),
                dma((ITERS, 2)),
                dma((2,)),
                dma((1,)),
                dma((NY,)),
                dma((1,)),
                dma((NY,)),
                dma((1,)),
                dma((NY,)),
            ],
            compiler_params=pltpu.CompilerParams(
                collective_id=0, has_side_effects=True, vmem_limit_bytes=16 * 2**20
            ),
        )(deltas, momentum, master)
        return pl.pallas_call(
            functools.partial(copy_kernel, len(outs)),
            out_shape=outs,
            in_specs=[pl.BlockSpec(memory_space=pltpu.VMEM)] * len(outs),
            out_specs=(anywhere,) * len(outs),
            scratch_shapes=[dma((len(outs),))],
            compiler_params=pltpu.CompilerParams(vmem_limit_bytes=16 * 2**20),
        )(*results)

    placed = (P("rep", "fsdp", None), P("fsdp", None), P("fsdp", None))
    return jax.shard_map(
        body,
        mesh=mesh,
        in_specs=placed,
        out_specs=(P("fsdp", None), P("fsdp", None), P()),
        check_vma=False,
    )
```

time: 87.6 us -> 81.1 us (0.926)
  Pallas kernels: 82.5 us -> 77.5 us
  local copies, waits for them, and re-layouts: 4.3 us -> 2.8 us
    pallas_call x1 -> x2, Pallas kernels: 82.5 us -> 77.5 us  [the longest x1 76.4 us: body(): pl.pallas_call(functools.partial(kernel, nf, nz), out_shape=outs, in_spec...]
    unnamed x5 -> x6, local copies, waits for them, and re-layouts: 4.3 us -> 2.8 us
where the time goes in v2:
time: 81.1 us; the launch traced here: 80.9 us
  Pallas kernels  77.5 us (96%)
  local copies, waits for them, and re-layouts  2.8 us (3%)
    pallas_call x1, Pallas kernels, body(): pl.pallas_call(functools.partial(kernel, nf, nz), out_shape=outs, in_spec...  76.4 us
    unnamed x6, local copies, waits for them, and re-layouts  2.8 us

profile of v2, /device:TPU:1, one launch (start us, length us, event | category | flops | bytes accessed | tf_op | source)
XLA Modules:
  0.0 80.9 jit_solution(17903494756869434140)
XLA Ops:
  0.6 0.0 copy-start
  0.6 0.9 %copy-done = f32[6,8192]{1,0:T(8,128)S(1)} copy-done((f32[6,8192]{1,0:T(8,128)S(1)}, f32[6,8192]{1,0:T(8,128)}, u32[]{:S(2)}) %copy-start) | copy-done | bytes 196632
  1.6 0.0 copy-start.1
  1.6 0.9 %copy-done.1 = f32[6,8192]{1,0:T(8,128)S(1)} copy-done((f32[6,8192]{1,0:T(8,128)S(1)}, f32[6,8192]{1,0:T(8,128)}, u32[]{:S(2)}) %copy-start.1) | copy-done | bytes 196632
  2.5 0.0 copy-start.2
  2.5 0.9 %copy-done.2 = bf16[1,6,8192]{2,1,0:T(8,128)(2,1)S(1)} copy-done((bf16[1,6,8192]{2,1,0:T(8,128)(2,1)S(1)}, bf16[1,6,8192]{2,1,0:T(8,128)(2,1)}, u32[]{:S(2)}) %copy-start.2) | copy-done | bytes 98328
  3.4 76.4 %shard_map.58 = (f32[6,8192]{1,0:T(8,128)S(1)}, f32[6,8192]{1,0:T(8,128)S(1)}, bf16[48,8192]{1,0:T(8,128)(2,1)S(1)}) custom-call(bf16[1,6,8192]{2,1,0:T(8,128)(2,1)S(1)} %copy-done.2, f32[6,8192]{1,0:T(8,128)S(1)} %copy-done, f32[6,8192]{1,0:T(8,128)S(1)} %copy-done.1), custom_call_target="tpu_custom_call" | custom-call | tf_op jit(solution)/shard_map/pallas_call | solution.py:284
  79.9 1.1 %shard_map.59 = (f32[6,8192]{1,0:T(8,128)}, f32[6,8192]{1,0:T(8,128)}, bf16[48,8192]{1,0:T(8,128)(2,1)}) custom-call(f32[6,8192]{1,0:T(8,128)S(1)} %get-tuple-element.6.refs_0_, f32[6,8192]{1,0:T(8,128)S(1)} %get-tuple-element.7.refs_1_, bf16[48,8192]{1,0:T(8,128)(2,1)S(1)} %get-tuple-element.8.refs_2_), custom_call_target="tpu_custom_call" | custom-call | tf_op jit(solution)/shard_map/pallas_call | solution.py:326
Async XLA Ops:
  0.6 1.0 %copy-start = (f32[6,8192]{1,0:T(8,128)S(1)}, f32[6,8192]{1,0:T(8,128)}, u32[]{:S(2)}) copy-start(f32[6,8192]{1,0:T(8,128)} %mom_in.1) | copy-start | bytes 589828
  1.6 0.9 %copy-start.1 = (f32[6,8192]{1,0:T(8,128)S(1)}, f32[6,8192]{1,0:T(8,128)}, u32[]{:S(2)}) copy-start(f32[6,8192]{1,0:T(8,128)} %mas_in.1) | copy-start | bytes 589828
  2.5 0.9 %copy-start.2 = (bf16[1,6,8192]{2,1,0:T(8,128)(2,1)S(1)}, bf16[1,6,8192]{2,1,0:T(8,128)(2,1)}, u32[]{:S(2)}) copy-start(bf16[1,6,8192]{2,1,0:T(8,128)(2,1)} %delta.1) | copy-start | bytes 294916

commit v3 on v2

--- a/solution.py
+++ b/solution.py
@@ -7,7 +7,6 @@
 from jax.experimental.pallas import tpu as pltpu
 from jax.sharding import PartitionSpec as P
 
-ITERS = 3
 EPS = 1e-06
 NY = 8
 LANES = 128
@@ -25,8 +24,8 @@
 
 def kernel(
     nf, nz, delta, mom_in, mas_in, nm_out, ns_out, fw_out,
-    own, mom, mas, nm, ns, fw, ra, rf, tb, zb, zq, ps, zs, cd, cn, nd, wb, wf,
-    local_sem, out_sem, a_sem, b_sem, p_sem, z_sem, cz_sem, cy_send, cy_recv, w_send, w_recv, v_send, v_recv,
+    own, mom, mas, nm, ns, fw, ra, rf, tb, zb, ps, zs, gm, gc, gs, gx, gy, gz, gf, gt, cd, cn, nd, wb, wf,
+    local_sem, out_sem, a_sem, b_sem, p_sem, z_sem, gc_sem, gx_sem, gy_sem, gz_sem, gf_sem, cz_send, cz_recv, cy_send, cy_recv, w_send, w_recv, v_send, v_recv,
 ):
     rows, width = own.shape
     block = width // NY
@@ -45,14 +44,16 @@
     sibling = (rep, f + 1 - 2 * core)
 
     def peers(axis, visit):
-        n = {"x": nf // 2, "y": NY, "z": nz, "plane": NY * nf}[axis]
-        me = {"x": x, "y": y, "z": z, "plane": plane}[axis]
+        n = {"x": nf // 2, "f": nf, "y": NY, "z": nz, "plane": NY * nf}[axis]
+        me = {"x": x, "f": f, "y": y, "z": z, "plane": plane}[axis]
 
         def step(i, carry):
             half = lax.div(i + 1, 2)
             place = lax.rem(me + n // 2 + half * (2 * lax.rem(i, 2) - 1) + n, n)
             if axis == "x":
                 device = (rep, 2 * place + core)
+            elif axis == "f":
+                device = (rep, place)
             elif axis == "y":
                 device = (z * NY + place, f)
             elif axis == "z":
@@ -110,14 +111,8 @@
 
         return total
 
-    def plane_stage(k, row):
-        return exchange("plane", NY * nf, plane, ps.at[k], p_sem.at[k], row)
-
-    def z_stage(k, row):
-        return exchange("z", nz, z, zs.at[k], z_sem.at[k], row)
-
     peers("y", send_a)
-    total = plane_stage(0, row)
+    total = exchange("plane", NY * nf, plane, ps, p_sem, row)
     mom_copy.start()
     mas_copy.start()
 
@@ -137,42 +132,109 @@
         return tb.at[lax.div(place, halves), :, columns]
 
     peers("z", lambda device, place: send(piece(place), zb.at[z], b_sem.at[0], b_sem.at[1], device))
-    total = z_stage(0, total())
+    total = exchange("z", nz, z, zs, z_sem, total())
     zb[z] = piece(z)[...]
-    zq[pl.ds(reps, LANES - reps), :] = jnp.zeros((LANES - reps, LANES), F32)
 
     row = total()
     drain(zb.at[pl.ds(0, nz - 1)], b_sem.at[1])
     held = zb[...].reshape(reps, chunk)
 
-    def center_of(squared):
+    def shares(squared):
         weight = jnp.where(lane < reps, 1.0 / jnp.sqrt(squared / entries + EPS), 0.0)
-        share = weight / jnp.sum(weight, axis=1, keepdims=True)
+        return weight / jnp.sum(weight, axis=1, keepdims=True)
+
+    def center_of(share):
         left = jnp.concatenate(split3(share), axis=0)[:, :reps]
         return jnp.sum(jnp.dot(left, held, preferred_element_type=F32), axis=0, keepdims=True)
 
-    def iterate(k, center):
-        spread = held.astype(F32) - center
-        spread = spread * spread
-        partial = spread[:, :LANES]
-        for part in range(1, parts):
-            partial = partial + spread[:, part * LANES : (part + 1) * LANES]
-        zq[pl.ds(0, reps), :] = partial
-        row = lax.dot_general(
-            jnp.ones((8, LANES), F32), zq[...], (((1,), (1,)), ((), ())),
+    half = reps // 2
+    spread = held.astype(F32) - center_of(shares(row))
+    first, second = spread[:half], spread[half:]
+    blank = jnp.zeros((LANES - reps, chunk), F32)
+
+    def products(left, *right):
+        return lax.dot_general(
+            left, jnp.concatenate((*right, blank), axis=0), (((1,), (1,)), ((), ())),
             precision=lax.Precision.HIGHEST, preferred_element_type=F32,
-        )[:1]
-        return center_of(z_stage(k, plane_stage(k, row)())())
-
-    center = lax.fori_loop(1, ITERS, iterate, center_of(row))
+        )
+
+    at_row = lax.broadcasted_iota(jnp.int32, (half, LANES), 0)
+    at_lane = lax.broadcasted_iota(jnp.int32, (half, LANES), 1)
+    upper, lower = products(first, second, first), products(second, first, second)
+    ends = jnp.sum(jnp.where(at_lane - half == at_row, lower, 0.0), axis=1, keepdims=True)
+    kept = jnp.where((at_lane < half) | (at_lane - half >= at_row), upper, lower)
+    kept = jnp.where(at_lane < reps, kept, jnp.where(at_lane == reps, ends, 0.0))
+
+    share_rows = half // nf
+    for g in range(nf):
+        gm[g % 2, g // 2] = kept[g * share_rows : (g + 1) * share_rows]
+    send(gm.at[1 - core], gc, gc_sem.at[0], gc_sem.at[1], sibling)
+    drain(gc, gc_sem.at[1])
+    gs[...] = gm[core] + gc[...]
+    gx[x] = gs[x]
+    peers("x", lambda device, place: send(gs.at[place], gx.at[x], gx_sem.at[0], gx_sem.at[1], device))
+    drain(gx.at[pl.ds(0, nf // 2 - 1)], gx_sem.at[1])
+    piece_sum = jnp.sum(gx[...], axis=0)
+    piece_sum = exchange("y", NY, y, gy, gy_sem, piece_sum)()
+    piece_sum = exchange("z", nz, z, gz, gz_sem, piece_sum)()
+    gf[f] = piece_sum
+    peers("f", lambda device, place: send(gf.at[f], gf.at[f], gf_sem.at[0], gf_sem.at[1], device))
+    drain(gf.at[pl.ds(0, nf - 1)], gf_sem.at[1])
+    for g in range(nf):
+        gt[pl.ds(g * share_rows, share_rows), :] = gf[g]
+
+    kept = gt[...]
+    same = at_lane == at_row
+
+    def to_row(column):
+        return jnp.sum(jnp.where(same, column, 0.0), axis=0, keepdims=True)
+
+    def to_column(line):
+        return jnp.sum(jnp.where(same, line, 0.0), axis=1, keepdims=True)
+
+    mixed = pltpu.roll(kept, LANES - half, 1)
+    between = jnp.where(at_lane < half, kept, 0.0)
+    upper = jnp.where((at_lane < half) & (at_lane >= at_row), mixed, 0.0)
+    lower = jnp.where(at_lane < at_row, mixed, 0.0)
+    ends_first = jnp.sum(jnp.where(same, mixed, 0.0), axis=0, keepdims=True)
+    ends_second = to_row(kept[:, reps : reps + 1])
+    squared = ends_first + pltpu.roll(ends_second, half, 1)
+    share = shares(squared)
+    share_first = jnp.where(lane < half, share, 0.0)
+    share_second = jnp.where(lane < half, pltpu.roll(share, LANES - half, 1), 0.0)
+    column_first, column_second = to_column(share_first), to_column(share_second)
+    with_first = (
+        jnp.sum(upper * column_first, axis=0, keepdims=True)
+        + to_row(jnp.sum(upper * share_first + between * share_second, axis=1, keepdims=True))
+        - ends_first * share_first
+    )
+    with_second = (
+        jnp.sum(between * column_first + lower * column_second, axis=0, keepdims=True)
+        + to_row(jnp.sum(lower * share_second, axis=1, keepdims=True))
+        + ends_second * share_second
+    )
+    along = with_first + pltpu.roll(with_second, half, 1)
+    squared = squared - 2.0 * along + jnp.sum(share * along, axis=1, keepdims=True)
+    center = center_of(shares(jnp.maximum(squared, 0.0)))
 
     for part in range(parts):
         cd[y, z, pl.ds(part, 1), :] = center[:, part * LANES : (part + 1) * LANES]
-    peers("z", lambda device, place: send(cd.at[y, z], cd.at[y, z], cz_sem.at[0], cz_sem.at[1], device))
+    peers("z", lambda device, place: send(cd.at[y, z], cd.at[y, z], cz_send.at[0], cz_recv.at[z], device))
+
+    def pass_on(i, carry):
+        half = lax.div(i, 2) + lax.rem(i, 2)
+        g = lax.rem(z + half * (1 - 2 * lax.rem(i, 2)) + nz, nz)
+
+        @pl.when(i > 0)
+        def _():
+            drain(cd.at[0, g], cz_recv.at[g])
+
+        peers("y", lambda device, place: send(cd.at[y, g], cd.at[y, g], cy_send.at[0], cy_recv.at[y], device))
+        return carry
+
+    lax.fori_loop(0, nz, pass_on, 0)
     mom_copy.wait()
     mas_copy.wait()
-    drain(cd.at[0, pl.ds(0, nz - 1)], cz_sem.at[1])
-    peers("y", lambda device, place: send(cd.at[y], cd.at[y], cy_send.at[0], cy_recv.at[y], device))
 
     def nearest(i):
         half = lax.div(i, 2) + lax.rem(i, 2)
@@ -248,10 +310,14 @@
     lax.fori_loop(0, NY, leave, 0)
     drain(ra.at[pl.ds(0, NY - 1)], a_sem.at[0])
     drain(zb.at[pl.ds(0, nz - 1)], b_sem.at[0])
-    for k in range(ITERS):
-        drain(ps.at[k, pl.ds(0, NY * nf - 1)], p_sem.at[k, 0])
-        drain(zs.at[k, pl.ds(0, nz - 1)], z_sem.at[k, 0])
-    drain(cd.at[0, pl.ds(0, nz - 1)], cz_sem.at[0])
+    drain(ps.at[pl.ds(0, NY * nf - 1)], p_sem.at[0])
+    drain(zs.at[pl.ds(0, nz - 1)], z_sem.at[0])
+    drain(gc, gc_sem.at[0])
+    drain(gx.at[pl.ds(0, nf // 2 - 1)], gx_sem.at[0])
+    drain(gy.at[pl.ds(0, NY - 1)], gy_sem.at[0])
+    drain(gz.at[pl.ds(0, nz - 1)], gz_sem.at[0])
+    drain(gf.at[pl.ds(0, nf - 1)], gf_sem.at[0])
+    drain(cd.at[0, pl.ds(0, nz - 1)], cz_send.at[0])
     drain(cd.at[pl.ds(0, NY - 1)], cy_send.at[0])
     drain(wb.at[pl.ds(0, nf // 2 - 1)], w_send.at[0])
     drain(wb.at[pl.ds(0, nf // 2)], v_send.at[0])
@@ -274,6 +340,7 @@
         block = width // NY
         chunk = block * rows // nz
         parts, tiles = chunk // LANES, block // LANES
+        share_rows = NY * nz // 2 // nf
         anywhere = pl.BlockSpec(memory_space=pl.ANY)
         dma = pltpu.SemaphoreType.DMA
         outs = (
@@ -297,9 +364,16 @@
                 pltpu.VMEM((tiles * NY * 8, LANES), F32),
                 pltpu.VMEM((rows, NY, block), BF16),
                 pltpu.VMEM((nz, NY, chunk), BF16),
-                pltpu.VMEM((LANES, LANES), F32),
-                pltpu.VMEM((ITERS, NY * nf, 1, LANES), F32),
-                pltpu.VMEM((ITERS, nz, 1, LANES), F32),
+                pltpu.VMEM((NY * nf, 1, LANES), F32),
+                pltpu.VMEM((nz, 1, LANES), F32),
+                pltpu.VMEM((2, nf // 2, share_rows, LANES), F32),
+                pltpu.VMEM((nf // 2, share_rows, LANES), F32),
+                pltpu.VMEM((nf // 2, share_rows, LANES), F32),
+                pltpu.VMEM((nf // 2, share_rows, LANES), F32),
+                pltpu.VMEM((NY, share_rows, LANES), F32),
+                pltpu.VMEM((nz, share_rows, LANES), F32),
+                pltpu.VMEM((nf, share_rows, LANES), F32),
+                pltpu.VMEM((nf * share_rows, LANES), F32),
                 pltpu.VMEM((NY, nz, parts, LANES), F32),
                 pltpu.VMEM((rows * tiles, LANES), F32),
                 pltpu.VMEM((rows * tiles, LANES), F32),
@@ -309,9 +383,15 @@
                 dma((3, NY)),
                 dma((2,)),
                 dma((2,)),
-                dma((ITERS, 2)),
-                dma((ITERS, 2)),
-                dma((2,)),
+                dma((2,)),
+                dma((2,)),
+                dma((2,)),
+                dma((2,)),
+                dma((2,)),
+                dma((2,)),
+                dma((2,)),
+                dma((1,)),
+                dma((nz,)),
                 dma((1,)),
                 dma((NY,)),
                 dma((1,)),
@@ -322,7 +402,7 @@
             compiler_params=pltpu.CompilerParams(
                 collective_id=0, has_side_effects=True, vmem_limit_bytes=16 * 2**20
             ),
-        )(deltas, momentum, master)
+        )(*(pltpu.with_memory_space_constraint(value, pltpu.HBM) for value in (deltas, momentum, master)))
         return pl.pallas_call(
             functools.partial(copy_kernel, len(outs)),
             out_shape=outs,

time: 81.1 us -> 71.8 us (0.89)
  Pallas kernels: 77.5 us -> 71.1 us
  local copies, waits for them, and re-layouts: 2.8 us -> 0 us
    pallas_call x1, Pallas kernels: 76.4 us -> 70 us  [body(): pl.pallas_call(functools.partial(kernel, nf, nz), out_shape=outs, in_spec...]
    unnamed x6 -> x0, local copies, waits for them, and re-layouts: 2.8 us -> none
where the time goes in v3:
time: 71.8 us; the launch traced here: 71.7 us
  Pallas kernels  71.1 us (99%)
    pallas_call x1, Pallas kernels, body(): pl.pallas_call(functools.partial(kernel, nf, nz), out_shape=outs, in_spec...  70 us

profile of v3, /device:TPU:1, one launch (start us, length us, event | category | flops | bytes accessed | tf_op | source)
XLA Modules:
  0.0 71.7 jit_solution(17931976160603440579)
XLA Ops:
  0.6 70.0 %shard_map.58 = (f32[6,8192]{1,0:T(8,128)S(1)}, f32[6,8192]{1,0:T(8,128)S(1)}, bf16[48,8192]{1,0:T(8,128)(2,1)S(1)}) custom-call(bf16[1,6,8192]{2,1,0:T(8,128)(2,1)} %delta.1, f32[6,8192]{1,0:T(8,128)} %mom_in.1, f32[6,8192]{1,0:T(8,128)} %mas_in.1), custom_call_target="tpu_custom_call" | custom-call | tf_op jit(solution)/shard_map/pallas_call | solution.py:351
  70.6 1.1 %shard_map.59 = (f32[6,8192]{1,0:T(8,128)}, f32[6,8192]{1,0:T(8,128)}, bf16[48,8192]{1,0:T(8,128)(2,1)}) custom-call(f32[6,8192]{1,0:T(8,128)S(1)} %get-tuple-element.6.refs_0_, f32[6,8192]{1,0:T(8,128)S(1)} %get-tuple-element.7.refs_1_, bf16[48,8192]{1,0:T(8,128)(2,1)S(1)} %get-tuple-element.8.refs_2_), custom_call_target="tpu_custom_call" | custom-call | tf_op jit(solution)/shard_map/pallas_call | solution.py:406

commit v4 on v3

--- a/solution.py
+++ b/solution.py
@@ -24,8 +24,8 @@
 
 def kernel(
     nf, nz, delta, mom_in, mas_in, nm_out, ns_out, fw_out,
-    own, mom, mas, nm, ns, fw, ra, rf, tb, zb, ps, zs, gm, gc, gs, gx, gy, gz, gf, gt, cd, cn, nd, wb, wf,
-    local_sem, out_sem, a_sem, b_sem, p_sem, z_sem, gc_sem, gx_sem, gy_sem, gz_sem, gf_sem, cz_send, cz_recv, cy_send, cy_recv, w_send, w_recv, v_send, v_recv,
+    own, mom, mas, nm, ns, fw, ra, rf, tb, zb, fs, ys, zs, gm, gx, gy, gz, gf, gt, cd, cn, nd, wb, wf,
+    local_sem, out_sem, a_sem, b_sem, f_sem, y_sem, z_sem, gx_sem, gy_sem, gz_sem, gf_sem, cz_send, cz_recv, cy_send, cy_recv, w_send, w_recv, v_send, v_recv,
 ):
     rows, width = own.shape
     block = width // NY
@@ -40,12 +40,11 @@
     y, z = lax.rem(rep, NY), lax.div(rep, NY)
 
     x, core = lax.div(f, 2), lax.rem(f, 2)
-    plane = y * nf + f
     sibling = (rep, f + 1 - 2 * core)
 
     def peers(axis, visit):
-        n = {"x": nf // 2, "f": nf, "y": NY, "z": nz, "plane": NY * nf}[axis]
-        me = {"x": x, "f": f, "y": y, "z": z, "plane": plane}[axis]
+        n = {"x": nf // 2, "f": nf, "y": NY, "z": nz}[axis]
+        me = {"x": x, "f": f, "y": y, "z": z}[axis]
 
         def step(i, carry):
             half = lax.div(i + 1, 2)
@@ -56,10 +55,8 @@
                 device = (rep, place)
             elif axis == "y":
                 device = (z * NY + place, f)
-            elif axis == "z":
+            else:
                 device = (place * NY + y, f)
-            else:
-                device = (z * NY + lax.div(place, nf), lax.rem(place, nf))
             visit(device, place)
             return carry
 
@@ -85,8 +82,9 @@
     def greet(device, place):
         pl.semaphore_signal(barrier, inc=1, device_id=device, device_id_type=MESH)
 
-    peers("plane", greet)
     peers("z", greet)
+    peers("y", greet)
+    peers("f", greet)
 
     mom_copy = pltpu.make_async_copy(mom_in, mom, local_sem.at[2])
     mas_copy = pltpu.make_async_copy(mas_in, mas, local_sem.at[3])
@@ -95,7 +93,7 @@
     value = own[...].astype(F32)
     squared = jnp.sum(jnp.sum(value * value, axis=0, keepdims=True), axis=1, keepdims=True)
     row = jnp.where(lane == rep, squared, 0.0)
-    pl.semaphore_wait(barrier, NY * nf + nz - 2)
+    pl.semaphore_wait(barrier, nz + NY + nf - 3)
 
     def send_a(device, place):
         columns = pl.ds(pl.multiple_of(place * block, block), block)
@@ -111,8 +109,9 @@
 
         return total
 
+    total = exchange("f", nf, f, fs, f_sem, row)
     peers("y", send_a)
-    total = exchange("plane", NY * nf, plane, ps, p_sem, row)
+    total = exchange("y", NY, y, ys, y_sem, total())
     mom_copy.start()
     mas_copy.start()
 
@@ -167,13 +166,10 @@
 
     share_rows = half // nf
     for g in range(nf):
-        gm[g % 2, g // 2] = kept[g * share_rows : (g + 1) * share_rows]
-    send(gm.at[1 - core], gc, gc_sem.at[0], gc_sem.at[1], sibling)
-    drain(gc, gc_sem.at[1])
-    gs[...] = gm[core] + gc[...]
-    gx[x] = gs[x]
-    peers("x", lambda device, place: send(gs.at[place], gx.at[x], gx_sem.at[0], gx_sem.at[1], device))
-    drain(gx.at[pl.ds(0, nf // 2 - 1)], gx_sem.at[1])
+        gm[g] = kept[g * share_rows : (g + 1) * share_rows]
+    gx[f] = gm[f]
+    peers("f", lambda device, place: send(gm.at[place], gx.at[f], gx_sem.at[0], gx_sem.at[1], device))
+    drain(gx.at[pl.ds(0, nf - 1)], gx_sem.at[1])
     piece_sum = jnp.sum(gx[...], axis=0)
     piece_sum = exchange("y", NY, y, gy, gy_sem, piece_sum)()
     piece_sum = exchange("z", nz, z, gz, gz_sem, piece_sum)()
@@ -310,10 +306,10 @@
     lax.fori_loop(0, NY, leave, 0)
     drain(ra.at[pl.ds(0, NY - 1)], a_sem.at[0])
     drain(zb.at[pl.ds(0, nz - 1)], b_sem.at[0])
-    drain(ps.at[pl.ds(0, NY * nf - 1)], p_sem.at[0])
+    drain(fs.at[pl.ds(0, nf - 1)], f_sem.at[0])
+    drain(ys.at[pl.ds(0, NY - 1)], y_sem.at[0])
     drain(zs.at[pl.ds(0, nz - 1)], z_sem.at[0])
-    drain(gc, gc_sem.at[0])
-    drain(gx.at[pl.ds(0, nf // 2 - 1)], gx_sem.at[0])
+    drain(gx.at[pl.ds(0, nf - 1)], gx_sem.at[0])
     drain(gy.at[pl.ds(0, NY - 1)], gy_sem.at[0])
     drain(gz.at[pl.ds(0, nz - 1)], gz_sem.at[0])
     drain(gf.at[pl.ds(0, nf - 1)], gf_sem.at[0])
@@ -364,12 +360,11 @@
                 pltpu.VMEM((tiles * NY * 8, LANES), F32),
                 pltpu.VMEM((rows, NY, block), BF16),
                 pltpu.VMEM((nz, NY, chunk), BF16),
-                pltpu.VMEM((NY * nf, 1, LANES), F32),
+                pltpu.VMEM((nf, 1, LANES), F32),
+                pltpu.VMEM((NY, 1, LANES), F32),
                 pltpu.VMEM((nz, 1, LANES), F32),
-                pltpu.VMEM((2, nf // 2, share_rows, LANES), F32),
-                pltpu.VMEM((nf // 2, share_rows, LANES), F32),
-                pltpu.VMEM((nf // 2, share_rows, LANES), F32),
-                pltpu.VMEM((nf // 2, share_rows, LANES), F32),
+                pltpu.VMEM((nf, share_rows, LANES), F32),
+                pltpu.VMEM((nf, share_rows, LANES), F32),
                 pltpu.VMEM((NY, share_rows, LANES), F32),
                 pltpu.VMEM((nz, share_rows, LANES), F32),
                 pltpu.VMEM((nf, share_rows, LANES), F32),

time: 71.8 us -> 70.2 us (0.978)
  Pallas kernels: 71.1 us -> 69.5 us
    pallas_call x1, Pallas kernels: 70 us -> 68.4 us  [body(): pl.pallas_call(functools.partial(kernel, nf, nz), out_shape=outs, in_spec...]
where the time goes in v4:
time: 70.2 us; the launch traced here: 70.1 us
  Pallas kernels  69.5 us (99%)
    pallas_call x1, Pallas kernels, body(): pl.pallas_call(functools.partial(kernel, nf, nz), out_shape=outs, in_spec...  68.4 us

profile of v4, /device:TPU:1, one launch (start us, length us, event | category | flops | bytes accessed | tf_op | source)
XLA Modules:
  0.0 70.1 jit_solution(17292728816155510256)
XLA Ops:
  0.6 68.4 %shard_map.58 = (f32[6,8192]{1,0:T(8,128)S(1)}, f32[6,8192]{1,0:T(8,128)S(1)}, bf16[48,8192]{1,0:T(8,128)(2,1)S(1)}) custom-call(bf16[1,6,8192]{2,1,0:T(8,128)(2,1)} %delta.1, f32[6,8192]{1,0:T(8,128)} %mom_in.1, f32[6,8192]{1,0:T(8,128)} %mas_in.1), custom_call_target="tpu_custom_call" | custom-call | tf_op jit(solution)/shard_map/pallas_call | solution.py:347
  69.0 1.1 %shard_map.59 = (f32[6,8192]{1,0:T(8,128)}, f32[6,8192]{1,0:T(8,128)}, bf16[48,8192]{1,0:T(8,128)(2,1)}) custom-call(f32[6,8192]{1,0:T(8,128)S(1)} %get-tuple-element.6.refs_0_, f32[6,8192]{1,0:T(8,128)S(1)} %get-tuple-element.7.refs_1_, bf16[48,8192]{1,0:T(8,128)(2,1)S(1)} %get-tuple-element.8.refs_2_), custom_call_target="tpu_custom_call" | custom-call | tf_op jit(solution)/shard_map/pallas_call | solution.py:401

commit v5 on v4

--- a/solution.py
+++ b/solution.py
@@ -25,7 +25,7 @@
 def kernel(
     nf, nz, delta, mom_in, mas_in, nm_out, ns_out, fw_out,
     own, mom, mas, nm, ns, fw, ra, rf, tb, zb, fs, ys, zs, gm, gx, gy, gz, gf, gt, cd, cn, nd, wb, wf,
-    local_sem, out_sem, a_sem, b_sem, f_sem, y_sem, z_sem, gx_sem, gy_sem, gz_sem, gf_sem, cz_send, cz_recv, cy_send, cy_recv, w_send, w_recv, v_send, v_recv,
+    z_answer, local_sem, out_sem, a_sem, b_sem, f_sem, y_sem, z_sem, gx_sem, gy_sem, gz_sem, gf_sem, cz_send, cz_recv, cy_send, cy_recv, w_send, w_recv, v_send, v_recv,
 ):
     rows, width = own.shape
     block = width // NY
@@ -79,12 +79,28 @@
 
     barrier = pltpu.get_barrier_semaphore()
 
-    def greet(device, place):
-        pl.semaphore_signal(barrier, inc=1, device_id=device, device_id_type=MESH)
-
-    peers("z", greet)
-    peers("y", greet)
-    peers("f", greet)
+    def above(visit):
+        def check(device, place):
+            @pl.when(place > z)
+            def _():
+                visit(device, place)
+
+        peers("z", check)
+
+    def below(visit):
+        def check(device, place):
+            @pl.when(place < z)
+            def _():
+                visit(device, place)
+
+        peers("z", check)
+
+    def tell(sem):
+        return lambda device, place: pl.semaphore_signal(sem, inc=1, device_id=device, device_id_type=MESH)
+
+    peers("y", tell(barrier))
+    above(tell(barrier))
+    peers("f", tell(barrier))
 
     mom_copy = pltpu.make_async_copy(mom_in, mom, local_sem.at[2])
     mas_copy = pltpu.make_async_copy(mas_in, mas, local_sem.at[3])
@@ -93,7 +109,8 @@
     value = own[...].astype(F32)
     squared = jnp.sum(jnp.sum(value * value, axis=0, keepdims=True), axis=1, keepdims=True)
     row = jnp.where(lane == rep, squared, 0.0)
-    pl.semaphore_wait(barrier, nz + NY + nf - 3)
+    pl.semaphore_wait(barrier, NY + nf - 2 + z)
+    below(tell(z_answer))
 
     def send_a(device, place):
         columns = pl.ds(pl.multiple_of(place * block, block), block)
@@ -109,8 +126,8 @@
 
         return total
 
+    peers("y", send_a)
     total = exchange("f", nf, f, fs, f_sem, row)
-    peers("y", send_a)
     total = exchange("y", NY, y, ys, y_sem, total())
     mom_copy.start()
     mas_copy.start()
@@ -130,7 +147,16 @@
         columns = pl.ds(pl.multiple_of(lax.rem(place, halves) * chunk, chunk), chunk)
         return tb.at[lax.div(place, halves), :, columns]
 
-    peers("z", lambda device, place: send(piece(place), zb.at[z], b_sem.at[0], b_sem.at[1], device))
+    def send_b(device, place):
+        send(piece(place), zb.at[z], b_sem.at[0], b_sem.at[1], device)
+
+    below(send_b)
+
+    @pl.when(z < nz - 1)
+    def _():
+        pl.semaphore_wait(z_answer, nz - 1 - z)
+
+    above(send_b)
     total = exchange("z", nz, z, zs, z_sem, total())
     zb[z] = piece(z)[...]
 
@@ -374,6 +400,7 @@
                 pltpu.VMEM((rows * tiles, LANES), F32),
                 pltpu.VMEM((nf, NY, rows * tiles, LANES), BF16),
                 pltpu.VMEM((tiles * nf * rows, LANES), F32),
+                pltpu.SemaphoreType.REGULAR,
                 dma((4,)),
                 dma((3, NY)),
                 dma((2,)),

time: 70.2 us -> 69.3 us (0.987)
  Pallas kernels: 69.5 us -> 68.6 us
    pallas_call x1, Pallas kernels: 68.4 us -> 67.5 us  [body(): pl.pallas_call(functools.partial(kernel, nf, nz), out_shape=outs, in_spec...]
where the time goes in v5:
time: 69.3 us; the launch traced here: 69.2 us
  Pallas kernels  68.6 us (99%)
    pallas_call x1, Pallas kernels, body(): pl.pallas_call(functools.partial(kernel, nf, nz), out_shape=outs, in_spec...  67.5 us

profile of v5, /device:TPU:1, one launch (start us, length us, event | category | flops | bytes accessed | tf_op | source)
XLA Modules:
  0.0 69.2 jit_solution(17143936636914705705)
XLA Ops:
  0.6 67.5 %shard_map.58 = (f32[6,8192]{1,0:T(8,128)S(1)}, f32[6,8192]{1,0:T(8,128)S(1)}, bf16[48,8192]{1,0:T(8,128)(2,1)S(1)}) custom-call(bf16[1,6,8192]{2,1,0:T(8,128)(2,1)} %delta.1, f32[6,8192]{1,0:T(8,128)} %mom_in.1, f32[6,8192]{1,0:T(8,128)} %mas_in.1), custom_call_target="tpu_custom_call" | custom-call | tf_op jit(solution)/shard_map/pallas_call | solution.py:373
  68.1 1.1 %shard_map.59 = (f32[6,8192]{1,0:T(8,128)}, f32[6,8192]{1,0:T(8,128)}, bf16[48,8192]{1,0:T(8,128)(2,1)}) custom-call(f32[6,8192]{1,0:T(8,128)S(1)} %get-tuple-element.6.refs_0_, f32[6,8192]{1,0:T(8,128)S(1)} %get-tuple-element.7.refs_1_, bf16[48,8192]{1,0:T(8,128)(2,1)S(1)} %get-tuple-element.8.refs_2_), custom_call_target="tpu_custom_call" | custom-call | tf_op jit(solution)/shard_map/pallas_call | solution.py:428

commit v6 on v5

--- a/solution.py
+++ b/solution.py
@@ -24,7 +24,7 @@
 
 def kernel(
     nf, nz, delta, mom_in, mas_in, nm_out, ns_out, fw_out,
-    own, mom, mas, nm, ns, fw, ra, rf, tb, zb, fs, ys, zs, gm, gx, gy, gz, gf, gt, cd, cn, nd, wb, wf,
+    own, mom, mas, nm, ns, ra, rf, tb, zb, fs, ys, zs, gm, gx, gy, gz, gf, gt, cd, cn, nd, wb, wf,
     z_answer, local_sem, out_sem, a_sem, b_sem, f_sem, y_sem, z_sem, gx_sem, gy_sem, gz_sem, gf_sem, cz_send, cz_recv, cy_send, cy_recv, w_send, w_recv, v_send, v_recv,
 ):
     rows, width = own.shape
@@ -138,19 +138,23 @@
         arrived = ra[k].astype(F32)
         for j in range(tiles):
             rf[pl.ds(8 * (j * NY + k), rows), :] = arrived[:, j * LANES : (j + 1) * LANES]
+
+    def piece(place):
+        columns = pl.ds(pl.multiple_of(lax.rem(place, halves) * chunk, chunk), chunk)
+        return tb.at[lax.div(place, halves), :, columns]
+
+    def send_b(device, place):
+        send(piece(place), zb.at[z], b_sem.at[0], b_sem.at[1], device)
+
     for r in range(rows):
         for j in range(tiles):
             column = pl.ds(j * LANES, LANES)
             tb[r, :, column] = rf[pl.ds(8 * j * NY + r, NY, stride=8), :].astype(BF16)
-
-    def piece(place):
-        columns = pl.ds(pl.multiple_of(lax.rem(place, halves) * chunk, chunk), chunk)
-        return tb.at[lax.div(place, halves), :, columns]
-
-    def send_b(device, place):
-        send(piece(place), zb.at[z], b_sem.at[0], b_sem.at[1], device)
-
-    below(send_b)
+        for place in range(r * halves, (r + 1) * halves):
+
+            @pl.when(place < z)
+            def _():
+                send_b((place * NY + y, f), place)
 
     @pl.when(z < nz - 1)
     def _():
@@ -266,7 +270,7 @@
         columns = pl.ds(pl.multiple_of(b * block, block), block)
         return [
             pltpu.make_async_copy(ref.at[:, columns], out.at[:, columns], out_sem.at[at, b])
-            for at, (ref, out) in enumerate(((nm, nm_out), (ns, ns_out), (fw, fw_out)))
+            for at, (ref, out) in enumerate(((nm, nm_out), (ns, ns_out)))
         ]
 
     def update(i, carry):
@@ -290,7 +294,7 @@
         wb[f, b] = nd[...].astype(BF16)
         peers("x", lambda device, place: send(wb.at[f, b], wb.at[f, b], w_send.at[0], w_recv.at[b], device))
         send(wb.at[f, b], wb.at[f, b], v_send.at[0], v_recv.at[b], sibling)
-        for copy in out_copies(b)[:2]:
+        for copy in out_copies(b):
             copy.start()
         return carry
 
@@ -318,8 +322,7 @@
                 wf[pl.ds(g * rows + r, tiles, stride=nf * rows), :] = dense[r * tiles : (r + 1) * tiles]
         for j in range(tiles):
             here = pl.ds(pl.multiple_of(b * block + j * LANES, LANES), LANES)
-            fw[:, here] = wf[pl.ds(j * nf * rows, nf * rows), :].astype(BF16)
-        out_copies(b)[2].start()
+            fw_out[:, here] = wf[pl.ds(j * nf * rows, nf * rows), :].astype(BF16)
         return carry
 
     lax.fori_loop(0, NY, place_weights, 0)
@@ -374,14 +377,13 @@
             functools.partial(kernel, nf, nz),
             out_shape=outs,
             in_specs=[pl.BlockSpec(memory_space=pltpu.HBM)] * 3,
-            out_specs=(anywhere,) * 3,
+            out_specs=(anywhere, anywhere, pl.BlockSpec(memory_space=pltpu.VMEM)),
             scratch_shapes=[
                 pltpu.VMEM((rows, width), BF16),
                 pltpu.VMEM((rows, width), F32),
                 pltpu.VMEM((rows, width), F32),
                 pltpu.VMEM((rows, width), F32),
                 pltpu.VMEM((rows, width), F32),
-                pltpu.VMEM((nf * rows, width), BF16),
                 pltpu.VMEM((NY, rows, block), BF16),
                 pltpu.VMEM((tiles * NY * 8, LANES), F32),
                 pltpu.VMEM((rows, NY, block), BF16),
@@ -402,7 +404,7 @@
                 pltpu.VMEM((tiles * nf * rows, LANES), F32),
                 pltpu.SemaphoreType.REGULAR,
                 dma((4,)),
-                dma((3, NY)),
+                dma((2, NY)),
                 dma((2,)),
                 dma((2,)),
                 dma((2,)),

time: 69.3 us -> 69.5 us (level)
  no operation moved by 1% of the time
where the time goes in v6:
time: 69.5 us; the launch traced here: 69.3 us
  Pallas kernels  68.7 us (99%)
    pallas_call x1, Pallas kernels, body(): pl.pallas_call(functools.partial(kernel, nf, nz), out_shape=outs, in_spec...  67.6 us

profile of v6, /device:TPU:1, one launch (start us, length us, event | category | flops | bytes accessed | tf_op | source)
XLA Modules:
  0.0 69.3 jit_solution(2132515492285070010)
XLA Ops:
  0.6 67.6 %shard_map.58 = (f32[6,8192]{1,0:T(8,128)S(1)}, f32[6,8192]{1,0:T(8,128)S(1)}, bf16[48,8192]{1,0:T(8,128)(2,1)S(1)}) custom-call(bf16[1,6,8192]{2,1,0:T(8,128)(2,1)} %delta.1, f32[6,8192]{1,0:T(8,128)} %mom_in.1, f32[6,8192]{1,0:T(8,128)} %mas_in.1), custom_call_target="tpu_custom_call" | custom-call | tf_op jit(solution)/shard_map/pallas_call | solution.py:376
  68.2 1.1 %shard_map.59 = (f32[6,8192]{1,0:T(8,128)}, f32[6,8192]{1,0:T(8,128)}, bf16[48,8192]{1,0:T(8,128)(2,1)}) custom-call(f32[6,8192]{1,0:T(8,128)S(1)} %get-tuple-element.6.refs_0_, f32[6,8192]{1,0:T(8,128)S(1)} %get-tuple-element.7.refs_1_, bf16[48,8192]{1,0:T(8,128)(2,1)S(1)} %get-tuple-element.8.refs_2_), custom_call_target="tpu_custom_call" | custom-call | tf_op jit(solution)/shard_map/pallas_call | solution.py:430
